TPU v7x, 256 devices: a whole 4x4x8 slice. The times are simulated.
256 devices in a mesh: dp: 64 (over y, z, core), tensor: 4 (over x).
Axes of the slice: x: 4, y: 4, z: 8, core: 2. Of those that a mesh axis runs over, the one named last changes fastest.
Arguments:
- activations: bfloat16 [32768, 8192], P('dp', 'tensor'), may hold values from -2000 to 2000
- norm_gain: float32 [8192], replicated, may hold values from 0.5 to 12
- w_query: bfloat16 [8192, 4096], P('dp', 'tensor'), may hold values from -0.0625 to 0.0625
- w_key: bfloat16 [8192, 512], P('dp', 'tensor'), may hold values from -0.0625 to 0.0625
- w_value: bfloat16 [8192, 512], P('dp', 'tensor'), may hold values from -0.0625 to 0.0625
- lengths: int32 [128], replicated, may hold values from 128 to 256
- languages: int32 [128], replicated, may hold values from 0 to 29
- lang_caps: int32 [30], replicated, may hold values from 128 to 256
- dest_shard: int32 [128], replicated, may hold values from 0 to 63, as said below
Outputs:
- attended: bfloat16 [32768, 4096], P('dp', 'tensor')
Inputs may be any that keep to these rules, and one draw needn't show every extreme that they name: `dest_shard`: every data shard receives exactly 2 documents.
All inputs are finite; a program needn't handle non-finite values.
Results may differ from a plain program's by a relative error of at most 0.007.
The roundings to bfloat16 on the way count: a program that leaves them out, or rounds other values in their place, can miss the bound.
Values may be sent and summed in bfloat16 or wider, within the bound.
A program may use at most 128 MiB of HBM per device.

v0:
```python
import math
import jax
import jax.numpy as jnp
from jax import lax
from jax.sharding import PartitionSpec as P

HEAD_WIDTH = 128
rope_base = 500000.0
norm_eps = 1e-05


def rotary_embedding(vectors, token_positions):
    half_width = vectors.shape[-1] // 2
    steps_range = jnp.arange(half_width, dtype=jnp.float32)
    frequency = jnp.exp(steps_range * (-2.0 * math.log(rope_base) / vectors.shape[-1]))
    angles = token_positions[..., None, None] * frequency
    cosine = jnp.cos(angles)
    sine_table = jnp.sin(angles)
    first_half = vectors[..., :half_width]
    second_half = vectors[..., half_width:]
    return jnp.concatenate(
        [
            first_half * cosine - second_half * sine_table,
            second_half * cosine + first_half * sine_table,
        ],
        axis=-1,
    )


def project(source_rows, norm_gain, w_query, w_key, w_value):
    gathered = lax.all_gather(source_rows, "tensor", axis=1, tiled=True)
    widened = gathered.astype(jnp.float32)
    row_scale = lax.rsqrt(jnp.mean(widened * widened, axis=1, keepdims=True) + norm_eps)
    normed = (widened * row_scale * norm_gain).astype(jnp.bfloat16)
    pieces = (
        lax.all_gather(w_query, "dp", axis=0, tiled=True),
        lax.all_gather(w_key, "dp", axis=0, tiled=True),
        lax.all_gather(w_value, "dp", axis=0, tiled=True),
    )
    return tuple(
        (
            jnp.dot(normed, weight_piece, preferred_element_type=jnp.float32)
            for weight_piece in pieces
        )
    )


def rotate_round(query_part, key_portion, value_portion, token_positions, head_dim):
    total_rows = query_part.shape[0]
    rotated_query = rotary_embedding(
        query_part.reshape(total_rows, -1, head_dim), token_positions
    ).reshape(total_rows, -1)
    rotated_key = rotary_embedding(
        key_portion.reshape(total_rows, -1, head_dim), token_positions
    ).reshape(total_rows, -1)
    return jnp.concatenate([rotated_query, rotated_key, value_portion], axis=1).astype(jnp.bfloat16)


def attend(packed, doc_lengths, query_width, key_width, head_dim, doc_max):
    total_rows = packed.shape[0]
    doc_total = total_rows // doc_max
    value_head_rows = key_width // head_dim
    heads_per_group = query_width // key_width
    queries = packed[:, :query_width].reshape(
        doc_total, doc_max, value_head_rows, heads_per_group, head_dim
    )
    key_rows = packed[:, query_width : query_width + key_width].reshape(
        doc_total, doc_max, value_head_rows, head_dim
    )
    value_rows = packed[:, query_width + key_width :].reshape(
        doc_total, doc_max, value_head_rows, head_dim
    )
    scores = jnp.einsum(
        "jqhgd,jkhd->jhgqk", queries, key_rows, preferred_element_type=jnp.float32
    ) / math.sqrt(head_dim)
    order_range = jnp.arange(doc_max)
    causal = order_range[:, None] >= order_range[None, :]
    scores = jnp.where(causal, scores, -jnp.inf)
    row_peak = jnp.max(scores, axis=-1, keepdims=True)
    exponent = jnp.exp(scores - row_peak)
    probability = (exponent / jnp.sum(exponent, axis=-1, keepdims=True)).astype(jnp.bfloat16)
    blended = jnp.einsum(
        "jhgqk,jkhd->jqhgd", probability, value_rows, preferred_element_type=jnp.float32
    )
    blended = blended.reshape(doc_total, doc_max, query_width)
    row_valid = order_range[None, :] < doc_lengths[:, None]
    result = jnp.where(row_valid[..., None], blended, 0.0)
    return result.reshape(total_rows, query_width).astype(jnp.bfloat16)


def local(
    activations, norm_gain, w_query, w_key, w_value, lengths, languages, lang_caps, dest_shard
):
    shard_count = lax.axis_size("dp")
    my_shard = lax.axis_index("dp")
    doc_count = lengths.shape[0]
    token_rows = activations.shape[0]
    rows_peer = token_rows // doc_count
    doc_max = rows_peer * shard_count
    docs_here = doc_count // shard_count
    head_dim = HEAD_WIDTH
    query_width = w_query.shape[1]
    key_width = w_key.shape[1]
    language_table = jnp.arange(lang_caps.shape[0])
    cap_of_doc = jnp.sum(
        jnp.where(languages[:, None] == language_table[None, :], lang_caps[None, :], 0), axis=1
    )
    capped = jnp.minimum(lengths, cap_of_doc)
    doc_order = jnp.arange(doc_count)
    same_dest = dest_shard[:, None] == dest_shard[None, :]
    doc_rank = jnp.sum(
        (same_dest & (doc_order[None, :] < doc_order[:, None])).astype(jnp.int32), axis=1
    )
    target_slot = dest_shard * docs_here + doc_rank
    holder = jnp.sum(
        jnp.where(doc_order[:, None] == target_slot[None, :], doc_order[None, :], 0), axis=1
    )
    mine = lax.dynamic_slice_in_dim(holder, my_shard * docs_here, docs_here)
    doc_lengths = jnp.take(capped, mine)
    holder_grid = jnp.transpose(holder.reshape(shard_count, docs_here))
    send_index = (
        holder_grid[:, None, :] * rows_peer + jnp.arange(rows_peer)[None, :, None]
    ).reshape(-1)
    outgoing = jnp.take(activations, send_index, axis=0).reshape(
        docs_here, rows_peer, shard_count, -1
    )
    arrived = lax.all_to_all(outgoing, "dp", split_axis=2, concat_axis=2, tiled=True)
    moved_rows = arrived.reshape(docs_here * doc_max, -1)
    query_part, key_portion, value_portion = project(moved_rows, norm_gain, w_query, w_key, w_value)
    token_positions = jnp.tile(jnp.arange(doc_max), docs_here).astype(jnp.float32)
    packed = rotate_round(query_part, key_portion, value_portion, token_positions, head_dim)
    return attend(packed, doc_lengths, query_width, key_width, head_dim, doc_max)


def solution(mesh):
    return jax.shard_map(
        local,
        mesh=mesh,
        in_specs=(
            P("dp", "tensor"),
            P(),
            P("dp", "tensor"),
            P("dp", "tensor"),
            P("dp", "tensor"),
            P(),
            P(),
            P(),
            P(),
        ),
        out_specs=P("dp", "tensor"),
        check_vma=False,
    )
```

profile of v0, /device:TPU:1, one launch (start us, length us, event | category | flops | bytes accessed | tf_op | source)
XLA Modules:
  0.0 453.7 jit_solution(18384676850716704676)
XLA Ops:
  6.5 1.0 convert_reduce_fusion
  7.5 0.7 multiply_add_fusion
  8.8 3.3 gather_fusion.1
  12.2 3.8 copy_select_fusion
  16.0 64.1 %all_to_all.5 = bf16[2,4,64,2048]{3,1,0,2:T(4,128)(2,1)S(1)} all-to-all(bf16[2,4,64,2048]{3,1,0,2:T(4,128)(2,1)S(1)} %copy_select_fusion), channel_id=1, replica_groups=mesh['dp'=64,'tensor'=4] {'dp'}, dimensions={2} | all-to-all | bytes 4194304 | tf_op jit(solution)/shard_map/all_to_all | solution.py:127
  80.1 2.5 copy.38
  82.7 0.7 all-gather.9.cloned.1.call-update
  83.5 0.7 all-gather.7.cloned.1.call-update
  85.0 0.6 gather_fusion
  85.8 1.0 multiply_cosine_fusion
  86.8 77.9 %all-gather.5.cloned.1.call-done = bf16[512,8192]{1,0:T(8,128)(2,1)} async-done(((bf16[512,2048]{1,0:T(8,128)(2,1)}), bf16[512,8192]{1,0:T(8,128)(2,1)}) %all-gather.5.cloned.1.call-update) | async-done | bytes 8388624 | tf_op jit(solution)/shard_map/all_gather | solution.py:31
  164.7 5.1 %fusion = f32[512]{0:T(512)S(1)} fusion(bf16[512,8192]{1,0:T(8,128)(2,1)} %all-gather.5.cloned.1.call-done), kind=kLoop, calls=%fused_computation.4 | loop fusion | flops 12582400 | bytes 8390656 | tf_op jit(solution)/shard_map/reduce_sum | solution.py:33
  169.8 76.8 %all-gather.9.cloned.1.call-done = bf16[8192,128]{1,0:T(8,128)(2,1)} async-done(((bf16[128,128]{1,0:T(8,128)(2,1)}), bf16[8192,128]{1,0:T(8,128)(2,1)}) %all-gather.9.cloned.1.call-update) | async-done | bytes 2097168 | tf_op jit(solution)/shard_map/all_gather | solution.py:37
  246.6 6.5 %convolution_bitcast_fusion.1 = f32[512,1,128]{0,2,1:T(8,128)S(1)} fusion(bf16[8192,128]{1,0:T(8,128)(2,1)} %all-gather.9.cloned.1.call-done, bf16[512,8192]{1,0:T(8,128)(2,1)} %all-gather.5.cloned.1.call-done, f32[8192]{0:T(1024)S(1)} %copy-done.1, f32[512]{0:T(512)S(1)} %add_rsqrt_fusion), kind=kOutput, calls=%fused_computation.22 | convolution fusion | flops 1090519040 | bytes 10782720 | tf_op jit(solution)/shard_map/dot_general | solution.py:42
  253.8 70.6 %all-gather.7.cloned.1.call-done = bf16[8192,128]{1,0:T(8,128)(2,1)} async-done(((bf16[128,128]{1,0:T(8,128)(2,1)}), bf16[8192,128]{1,0:T(8,128)(2,1)}) %all-gather.7.cloned.1.call-update) | async-done | bytes 2097168 | tf_op jit(solution)/shard_map/all_gather | solution.py:38
  324.4 6.4 %convolution_convert_fusion = bf16[512,128]{1,0:T(8,128)(2,1)S(1)} fusion(bf16[8192,128]{1,0:T(8,128)(2,1)} %all-gather.7.cloned.1.call-done, bf16[512,8192]{1,0:T(8,128)(2,1)} %all-gather.5.cloned.1.call-done, f32[8192]{0:T(1024)S(1)} %copy-done.1, f32[512]{0:T(512)S(1)} %add_rsqrt_fusion), kind=kOutput, calls=%fused_computation.23 | convolution fusion | flops 1090584576 | bytes 10651648 | tf_op jit(solution)/shard_map/dot_general | solution.py:42
  330.8 93.0 %all-gather.11.cloned.1.call-done = bf16[8192,1024]{1,0:T(8,128)(2,1)} async-done(((bf16[128,1024]{1,0:T(8,128)(2,1)}), bf16[8192,1024]{1,0:T(8,128)(2,1)}) %all-gather.11.cloned.1.call-update) | async-done | bytes 16777232 | tf_op jit(solution)/shard_map/all_gather | solution.py:36
  423.8 14.5 %convolution_bitcast_fusion = f32[64,8,8,128]{3,1,2,0:T(8,128)S(1)} fusion(bf16[8192,1024]{1,0:T(8,128)(2,1)} %all-gather.11.cloned.1.call-done, bf16[512,8192]{1,0:T(8,128)(2,1)} %all-gather.5.cloned.1.call-done, f32[8192]{0:T(1024)S(1)} %copy-done.1, f32[512]{0:T(512)S(1)} %add_rsqrt_fusion), kind=kOutput, calls=%fused_computation.21 | convolution fusion | flops 8606711808 | bytes 27297792 | tf_op jit(solution)/shard_map/dot_general | solution.py:42
  438.8 0.9 subtract_convert_fusion
  440.3 0.8 fusion.4
  441.0 0.9 fusion.3
  441.9 2.3 fusion.9
  444.2 1.7 copy.43
  445.9 1.2 fusion.5
  (43 shorter events, 3.4 us)
Async XLA Ops:
  6.5 2.3 copy-start
  6.5 158.2 %all-gather.5.cloned.1.call-start = ((), (), s32[]{:S(2)}) async-start(), calls=%async_computation.1 | async-start | bytes 10485760 | tf_op jit(solution)/shard_map/all_gather | solution.py:31
  80.1 4.6 %copy-start.2 = (s32[30]{0:T(128)S(1)}, s32[30]{0:T(128)}, u32[]{:S(2)}) copy-start(s32[30]{0:T(128)} %param.16) | copy-start | bytes 364
  80.1 4.6 %copy-start.3 = (s32[128]{0:T(128)S(1)}, s32[128]{0:T(128)}, u32[]{:S(2)}) copy-start(s32[128]{0:T(128)} %param.15) | copy-start | bytes 1540
  80.1 4.7 %copy-start.4 = (s32[128]{0:T(128)S(1)}, s32[128]{0:T(128)}, u32[]{:S(2)}) copy-start(s32[128]{0:T(128)} %param.14) | copy-start | bytes 1540
  82.7 164.0 %all-gather.9.cloned.1.call-start = ((), (), s32[]{:S(2)}) async-start(), calls=%async_computation.3 | async-start | bytes 2129920 | tf_op jit(solution)/shard_map/all_gather | solution.py:37
  83.4 241.0 %all-gather.7.cloned.1.call-start = ((), (), s32[]{:S(2)}) async-start(), calls=%async_computation.2 | async-start | bytes 2129920 | tf_op jit(solution)/shard_map/all_gather | solution.py:38
  84.2 339.6 %all-gather.11.cloned.1.call-start = ((), (), s32[]{:S(2)}) async-start(), calls=%async_computation.4 | async-start | bytes 17039360 | tf_op jit(solution)/shard_map/all_gather | solution.py:36
  86.8 159.8 %copy-start.1 = (f32[8192]{0:T(1024)S(1)}, f32[8192]{0:T(1024)}, u32[]{:S(2)}) copy-start(f32[8192]{0:T(1024)} %param.10) | copy-start | bytes 98308
Sparse Core Ops, SparseCore 0:
  82.8 81.8 all-gather.4
  167.5 79.0 all-gather.8
  249.4 74.9 all-gather.6
  327.1 96.6 all-gather.10
where the time goes:
time: 454 us
  waiting for transfers between devices  320 us (70%)
  blocking collectives  64.1 us (14%)
  matrix products  30.4 us (7%)
  other arithmetic  16.2 us (4%)
  between operations  13.3 us (3%)
  local copies, waits for them, and re-layouts  9.25 us (2%)
    all_gather x1, waiting for transfers between devices, project(): lax.all_gather(w_query, 'dp', axis=0, tiled=True)  93 us
    all_gather x1, waiting for transfers between devices, project(): gathered = lax.all_gather(source_rows, 'tensor', axis=1, tiled=True)  77.9 us
    all_gather x1, waiting for transfers between devices, project(): lax.all_gather(w_key, 'dp', axis=0, tiled=True)  76.8 us
    all_gather x1, waiting for transfers between devices, project(): lax.all_gather(w_value, 'dp', axis=0, tiled=True)  70.6 us
    all_to_all x1, blocking collectives, local(): lax.all_to_all(outgoing, 'dp', split_axis=2, concat_axis=2, tiled=True)  64.1 us
    dot_general x3, matrix products, project(): jnp.dot(normed, weight_piece, preferred_element_type=jnp.float32)  27.4 us
  transfers between devices with their start and end apart: 4, of which 4 were waited for; matrix products, arithmetic and copies ran while one was open for 5% of the time, Pallas kernels for 0%

commit v1 on v0

--- a/solution.py
+++ b/solution.py
@@ -7,6 +7,11 @@
 HEAD_WIDTH = 128
 rope_base = 500000.0
 norm_eps = 1e-05
+
+
+def all_by_exchange(x, name, dim):
+    sent = jnp.stack([x] * lax.axis_size(name))
+    return jnp.concatenate(lax.all_to_all(sent, name, 0, 0), axis=dim)
 
 
 def rotary_embedding(vectors, token_positions):
@@ -34,7 +39,7 @@
     normed = (widened * row_scale * norm_gain).astype(jnp.bfloat16)
     pieces = (
         lax.all_gather(w_query, "dp", axis=0, tiled=True),
-        lax.all_gather(w_key, "dp", axis=0, tiled=True),
+        all_by_exchange(w_key, "dp", 0),
         lax.all_gather(w_value, "dp", axis=0, tiled=True),
     )
     return tuple(

time: 454 us -> 376 us (0.83)
  waiting for transfers between devices: 320 us -> 235 us
  starting transfers between devices: 0.12 us -> 6.11 us
    all_gather x1 -> x0, waiting for transfers between devices: 76.8 us -> none  [project(): lax.all_gather(w_key, 'dp', axis=0, tiled=True)]
    all_gather x1, waiting for transfers between devices: 77.9 us -> 70.6 us  [project(): gathered = lax.all_gather(source_rows, 'tensor', axis=1, tiled=True)]
    all_to_all x0 -> x1, starting transfers between devices: none -> 6.03 us  [all_by_exchange(): return jnp.concatenate(lax.all_to_all(sent, name, 0, 0), axis=dim)]
  transfers between devices with their start and end apart: 4 -> 4, of which waited for: 4 -> 3; matrix products, arithmetic and copies ran while one was open for 5% -> 6% of each run, Pallas kernels for 0% -> 0%
where the time goes in v1:
time: 376 us
  waiting for transfers between devices  235 us (62%)
  blocking collectives  64.1 us (17%)
  matrix products  30.6 us (8%)
  other arithmetic  16.2 us (4%)
  between operations  13.3 us (4%)
  local copies, waits for them, and re-layouts  11 us (3%)
  starting transfers between devices  6.11 us (2%)
    all_gather x1, waiting for transfers between devices, project(): lax.all_gather(w_query, 'dp', axis=0, tiled=True)  93.1 us
    all_gather x1, waiting for transfers between devices, project(): gathered = lax.all_gather(source_rows, 'tensor', axis=1, tiled=True)  70.6 us
    all_gather x1, waiting for transfers between devices, project(): lax.all_gather(w_value, 'dp', axis=0, tiled=True)  69.6 us
    all_to_all x1, blocking collectives, local(): lax.all_to_all(outgoing, 'dp', split_axis=2, concat_axis=2, tiled=True)  64.1 us
    dot_general x3, matrix products, project(): jnp.dot(normed, weight_piece, preferred_element_type=jnp.float32)  27.6 us
  transfers between devices with their start and end apart: 4, of which 3 were waited for; matrix products, arithmetic and copies ran while one was open for 6% of the time, Pallas kernels for 0%

profile of v1, /device:TPU:1, one launch (start us, length us, event | category | flops | bytes accessed | tf_op | source)
XLA Modules:
  0.0 376.2 jit_solution(10887657832484510054)
XLA Ops:
  6.5 1.0 convert_reduce_fusion
  7.5 0.7 multiply_add_fusion
  8.8 3.3 gather_fusion.1
  12.2 3.8 %copy_select_fusion = bf16[2,4,64,2048]{3,1,0,2:T(4,128)(2,1)S(1)} fusion(bf16[2,4,64,2048]{3,2,1,0:T(8,128)(2,1)} %bitcast.61, pred[2,4,64]{1,0,2:T(4,128)(4,1)S(1)} %copy.36), kind=kLoop, calls=%fused_computation.16 | loop fusion | flops 1048576 | bytes 4194816 | tf_op jit(solution)/shard_map/jit(_take)/select_n | solution.py:129
  16.0 64.1 %all_to_all.10 = bf16[2,4,64,2048]{3,1,0,2:T(4,128)(2,1)S(1)} all-to-all(bf16[2,4,64,2048]{3,1,0,2:T(4,128)(2,1)S(1)} %copy_select_fusion), channel_id=1, replica_groups=mesh['dp'=64,'tensor'=4] {'dp'}, dimensions={2} | all-to-all | bytes 4194304 | tf_op jit(solution)/shard_map/all_to_all | solution.py:132
  80.1 2.5 copy.38
  82.7 0.7 all-gather.6.cloned.1.call-update
  83.4 0.7 all-gather.8.cloned.1.call-update
  84.1 1.8 stack.2
  86.0 6.0 %all-to-all-start.1 = ((bf16[64,128,128]{2,1,0:T(8,128)(2,1)}), bf16[64,128,128]{2,1,0:T(8,128)(2,1)}, u32[]{:S(2)}, u32[]{:S(2)}) async-start(bf16[64,128,128]{2,1,0:T(8,128)(2,1)} %stack.2), calls=%async_computation.1 | async-start | bytes 4194304 | tf_op jit(solution)/shard_map/all_to_all | solution.py:14
  93.1 1.0 multiply_cosine_fusion
  94.1 70.6 %all-gather.4.cloned.1.call-done = bf16[512,8192]{1,0:T(8,128)(2,1)} async-done(((bf16[512,2048]{1,0:T(8,128)(2,1)}), bf16[512,8192]{1,0:T(8,128)(2,1)}) %all-gather.4.cloned.1.call-update) | async-done | bytes 8388624 | tf_op jit(solution)/shard_map/all_gather | solution.py:36
  164.7 5.1 %fusion = f32[512]{0:T(512)S(1)} fusion(bf16[512,8192]{1,0:T(8,128)(2,1)} %all-gather.4.cloned.1.call-done), kind=kLoop, calls=%fused_computation.4 | loop fusion | flops 12582400 | bytes 8390656 | tf_op jit(solution)/shard_map/reduce_sum | solution.py:38
  169.8 6.5 %convolution_bitcast_fusion.1 = f32[512,1,128]{0,2,1:T(8,128)S(1)} fusion(bf16[8192,128]{1,0:T(8,128)(2,1)} %bitcast.6, bf16[512,8192]{1,0:T(8,128)(2,1)} %all-gather.4.cloned.1.call-done, f32[8192]{0:T(1024)S(1)} %copy-done.2, f32[512]{0:T(512)S(1)} %add_rsqrt_fusion), kind=kOutput, calls=%fused_computation.22 | convolution fusion | flops 1090519040 | bytes 10782720 | tf_op jit(solution)/shard_map/dot_general | solution.py:47
  177.0 69.6 %all-gather.6.cloned.1.call-done = bf16[8192,128]{1,0:T(8,128)(2,1)} async-done(((bf16[128,128]{1,0:T(8,128)(2,1)}), bf16[8192,128]{1,0:T(8,128)(2,1)}) %all-gather.6.cloned.1.call-update) | async-done | bytes 2097168 | tf_op jit(solution)/shard_map/all_gather | solution.py:43
  246.6 6.4 %convolution_convert_fusion = bf16[512,128]{1,0:T(8,128)(2,1)S(1)} fusion(bf16[8192,128]{1,0:T(8,128)(2,1)} %all-gather.6.cloned.1.call-done, bf16[512,8192]{1,0:T(8,128)(2,1)} %all-gather.4.cloned.1.call-done, f32[8192]{0:T(1024)S(1)} %copy-done.2, f32[512]{0:T(512)S(1)} %add_rsqrt_fusion), kind=kOutput, calls=%fused_computation.23 | convolution fusion | flops 1090584576 | bytes 10651648 | tf_op jit(solution)/shard_map/dot_general | solution.py:47
  253.0 93.1 %all-gather.8.cloned.1.call-done = bf16[8192,1024]{1,0:T(8,128)(2,1)} async-done(((bf16[128,1024]{1,0:T(8,128)(2,1)}), bf16[8192,1024]{1,0:T(8,128)(2,1)}) %all-gather.8.cloned.1.call-update) | async-done | bytes 16777232 | tf_op jit(solution)/shard_map/all_gather | solution.py:41
  346.1 14.7 %convolution_bitcast_fusion = f32[64,8,8,128]{3,1,2,0:T(8,128)S(1)} fusion(bf16[8192,1024]{1,0:T(8,128)(2,1)} %all-gather.8.cloned.1.call-done, bf16[512,8192]{1,0:T(8,128)(2,1)} %all-gather.4.cloned.1.call-done, f32[8192]{0:T(1024)S(1)} %copy-done.2, f32[512]{0:T(512)S(1)} %add_rsqrt_fusion), kind=kOutput, calls=%fused_computation.21 | convolution fusion | flops 8606711808 | bytes 27297792 | tf_op jit(solution)/shard_map/dot_general | solution.py:47
  361.3 0.9 subtract_convert_fusion
  362.8 0.8 fusion.4
  363.6 0.9 fusion.3
  364.4 2.3 fusion.9
  366.7 1.7 copy.43
  368.4 1.2 fusion.5
  (45 shorter events, 3.5 us)
Async XLA Ops:
  6.5 2.3 copy-start
  6.5 158.2 %all-gather.4.cloned.1.call-start = ((), (), s32[]{:S(2)}) async-start(), calls=%async_computation.2 | async-start | bytes 10485760 | tf_op jit(solution)/shard_map/all_gather | solution.py:36
  80.1 4.0 %copy-start.1 = (bf16[128,128]{1,0:T(8,128)(2,1)S(1)}, bf16[128,128]{1,0:T(8,128)(2,1)}, u32[]{:S(2)}) copy-start(bf16[128,128]{1,0:T(8,128)(2,1)} %param.12) | copy-start | bytes 98308
  82.6 9.4 %copy-start.3 = (s32[30]{0:T(128)S(1)}, s32[30]{0:T(128)}, u32[]{:S(2)}) copy-start(s32[30]{0:T(128)} %param.16) | copy-start | bytes 364
  82.6 9.4 %copy-start.4 = (s32[128]{0:T(128)S(1)}, s32[128]{0:T(128)}, u32[]{:S(2)}) copy-start(s32[128]{0:T(128)} %param.15) | copy-start | bytes 1540
  82.6 9.5 %copy-start.5 = (s32[128]{0:T(128)S(1)}, s32[128]{0:T(128)}, u32[]{:S(2)}) copy-start(s32[128]{0:T(128)} %param.14) | copy-start | bytes 1540
  82.6 164.0 %all-gather.6.cloned.1.call-start = ((), (), s32[]{:S(2)}) async-start(), calls=%async_computation.3 | async-start | bytes 2129920 | tf_op jit(solution)/shard_map/all_gather | solution.py:43
  83.4 262.7 %all-gather.8.cloned.1.call-start = ((), (), s32[]{:S(2)}) async-start(), calls=%async_computation.4 | async-start | bytes 17039360 | tf_op jit(solution)/shard_map/all_gather | solution.py:41
  86.0 83.9 %all-to-all-start.1 = ((bf16[64,128,128]{2,1,0:T(8,128)(2,1)}), bf16[64,128,128]{2,1,0:T(8,128)(2,1)}, u32[]{:S(2)}, u32[]{:S(2)}) async-start(bf16[64,128,128]{2,1,0:T(8,128)(2,1)} %stack.2), calls=%async_computation.1 | async-start | bytes 4194304 | tf_op jit(solution)/shard_map/all_to_all | solution.py:14
  94.1 75.7 %copy-start.2 = (f32[8192]{0:T(1024)S(1)}, f32[8192]{0:T(1024)}, u32[]{:S(2)}) copy-start(f32[8192]{0:T(1024)} %param.10) | copy-start | bytes 98308
Sparse Core Ops, SparseCore 0:
  82.8 81.8 all-gather.3
  167.5 79.0 all-gather.5
  249.4 96.6 all-gather.7
